TPU v7x, 32 devices: a whole 2x2x4 slice. The times are simulated.
32 devices in a mesh: groups: 2 (over x), cache: 16 (over z, y, core).
Axes of the slice: x: 2, y: 2, z: 4, core: 2. Of those that a mesh axis runs over, the one named last changes fastest.
Arguments:
- prefix_len: int32 [32], P('groups'), parts along dimension 0, may hold values from 128 to 1024, as said below
- hits: int32 [32, 1], P('groups'), parts along dimension 0, may hold values from 0 to 15, as said below
- span_block: int32 [32, 16], P('groups'), parts along dimension 0, may hold values from 0 to 15, each once within a row
- queries: bfloat16 [2048, 2048], P(('groups', 'cache')), parts along dimension 0, may hold values from -100 to 100
- fresh_keys: bfloat16 [2048, 128], P(('groups', 'cache')), parts along dimension 0, may hold values from -4 to 4
- fresh_values: bfloat16 [2048, 128], P(('groups', 'cache')), parts along dimension 0, may hold values from -4 to 4
- cache_keys: bfloat16 [65536, 128], P(('groups', 'cache')), parts along dimension 0, may hold values from -4 to 4
- cache_values: bfloat16 [65536, 128], P(('groups', 'cache')), parts along dimension 0, may hold values from -4 to 4
Outputs:
- attended: bfloat16 [2048, 2048], P(('groups', 'cache')), parts along dimension 0
There are 2 independent parts, one for each index of `groups`. A program takes and returns all parts, laid end to end along the dimension named above; each array names one. Nothing has to cross between parts.
Inputs may be any that keep to these rules, and one draw needn't show every extreme that they name: `prefix_len`: every request's prefix holds at least 128 tokens, and one request in every draw holds exactly 1024. `hits`: each row names 1 different devices. Each device is named by at most 2 requests; 4 devices are named by exactly 2, half of them by one, a quarter by none. `span_block`: each row is a permutation.
All inputs are finite; a program needn't handle non-finite values.
Results may differ from a plain program's by a relative error of at most 0.0065.
Values may be sent and summed in bfloat16 or wider, within the bound.
A program may use at most 64 MiB of HBM per device.

v0:
```python
import math

import jax
import jax.numpy as jnp
from jax import lax
from jax.sharding import PartitionSpec as P

HEADS = 16
HD = 128
PAGE = 128
CAP = 2
REQUESTS = 16
TOK_REQ = 4
PAGES_DEV = 16


floor_score = -1e30


def owner_block(query_block, page_keys, page_values, visible):
    scale = HD ** (-0.5)
    scores = (
        jnp.einsum("thd,kd->thk", query_block, page_keys, preferred_element_type=jnp.float32)
        * scale
    )
    scores = jnp.where(visible, scores, floor_score)
    maxima = jnp.max(scores, axis=2)
    weights = jnp.exp(scores - maxima[:, :, None]) * visible
    totals = jnp.maximum(jnp.sum(weights, axis=2), 1.0)
    summed = jnp.einsum(
        "thk,kd->thd", weights.astype(jnp.bfloat16), page_values, preferred_element_type=jnp.float32
    )
    partial_out = (summed / totals[:, :, None]).astype(jnp.bfloat16)
    return (partial_out, maxima + jnp.log(totals))


def serve_slots(slot_queries, slot_keys, slot_values, slot_visible, devices):
    per_group = math.gcd(devices, 16)

    def one_slot(packed):
        queries_in, page_keys, page_values, visible = packed
        grouped = queries_in.reshape(devices // per_group, per_group * TOK_REQ, HEADS, HD)

        def one_group(query_block):
            return owner_block(query_block, page_keys, page_values, visible)

        outputs, lse_rows = lax.map(one_group, grouped)
        return (
            outputs.reshape(devices, TOK_REQ, HEADS * HD),
            lse_rows.reshape(devices, TOK_REQ, HEADS),
        )

    return lax.map(one_slot, (slot_queries, slot_keys, slot_values, slot_visible))


def body(prefix_len, hits, span_block, queries, fresh_keys, fresh_values, cache_keys, cache_values):
    devices = lax.axis_size("cache")
    myself = lax.axis_index("cache")
    hit_count = hits.shape[1]
    region = PAGES_DEV // CAP * PAGE
    per_device = REQUESTS * TOK_REQ
    scale = HD ** (-0.5)
    offsets = jnp.arange(TOK_REQ, dtype=jnp.int32)
    request_ids = jnp.arange(REQUESTS, dtype=jnp.int32)
    owner_ids = jnp.arange(devices, dtype=jnp.int32)
    slot_ids = jnp.arange(CAP, dtype=jnp.int32)
    is_named = jnp.any(hits[:, :, None] == owner_ids[None, None, :], axis=1).astype(jnp.int32)
    earlier = (request_ids[None, :] < request_ids[:, None]).astype(jnp.int32)
    slot_rank = jnp.sum(earlier[:, :, None] * is_named[None, :, :], axis=1)
    holding = (is_named[None] == 1) & (slot_rank[None] == slot_ids[:, None, None])
    occupied = jnp.any(holding, axis=1)
    send_request = jnp.sum(holding * request_ids[None, :, None], axis=1)
    local_request = jnp.take(send_request, myself, axis=1)
    local_occupied = jnp.take(occupied, myself, axis=1)
    local_hits = jnp.take(hits, local_request, axis=0)
    hit_place = jnp.sum(
        jnp.where(local_hits == myself, jnp.arange(hit_count, dtype=jnp.int32)[None, :], 0), axis=1
    )
    page_limit = jnp.take(prefix_len, local_request)
    prefix_spot = hit_place[:, None] * region + jnp.arange(region, dtype=jnp.int32)[None, :]
    slot_visible = local_occupied[:, None] & (prefix_spot < page_limit[:, None])
    region_keys = cache_keys.reshape(CAP, region, HD)
    region_values = cache_values.reshape(CAP, region, HD)
    query_heads = queries.reshape(REQUESTS, TOK_REQ, HEADS, HD)
    my_blocks = jnp.take(span_block, myself, axis=1)
    query_spot = my_blocks[:, None] * TOK_REQ + offsets[None, :]
    running = jnp.full((REQUESTS, TOK_REQ, HEADS), floor_score, jnp.float32)
    key_piece = lax.all_gather(fresh_keys, "cache", axis=0, tiled=True)
    value_piece = lax.all_gather(fresh_values, "cache", axis=0, tiled=True)
    count = key_piece.shape[0] // per_device
    key_rows = jnp.transpose(key_piece.reshape(count, REQUESTS, TOK_REQ, HD), (1, 0, 2, 3)).reshape(
        REQUESTS, count * TOK_REQ, HD
    )
    value_rows = jnp.transpose(
        value_piece.reshape(count, REQUESTS, TOK_REQ, HD), (1, 0, 2, 3)
    ).reshape(REQUESTS, count * TOK_REQ, HD)
    key_spot = (span_block[:, :, None] * TOK_REQ + offsets[None, None, :]).reshape(
        REQUESTS, count * TOK_REQ
    )
    visible = (key_spot[:, None, :] <= query_spot[:, :, None])[:, :, None, :]
    scores = (
        jnp.einsum("rthd,rkd->rthk", query_heads, key_rows, preferred_element_type=jnp.float32)
        * scale
    )
    scores = jnp.where(visible, scores, floor_score)
    highest = jnp.maximum(running, jnp.max(scores, axis=3))
    weights = jnp.exp(scores - highest[..., None]) * visible
    totals = jnp.sum(weights, axis=3)
    value_wide = value_rows.astype(jnp.float32)
    summed = jnp.einsum("rthk,rkd->rthd", weights, value_wide, precision=lax.Precision.HIGHEST)
    running, totals, summed = (highest, totals, summed)
    prompt_out = summed / totals[..., None]
    prompt_lse = running + jnp.log(totals)
    units = queries.reshape(REQUESTS, TOK_REQ, HEADS * HD)
    outgoing = jnp.take(units, send_request, axis=0)
    arrived_queries = lax.all_to_all(outgoing, "cache", split_axis=1, concat_axis=1, tiled=True)
    partial_out, partial_lse = serve_slots(
        arrived_queries, region_keys, region_values, slot_visible, devices
    )
    returned_out, returned_lse = (
        lax.all_to_all(
            partial_out.astype(jnp.float32), "cache", split_axis=1, concat_axis=1, tiled=True
        ).astype(partial_out.dtype),
        lax.all_to_all(partial_lse, "cache", split_axis=1, concat_axis=1, tiled=True),
    )
    flat_out = returned_out.reshape(CAP * devices, TOK_REQ, HEADS, HD)
    flat_lse = returned_lse.reshape(CAP * devices, TOK_REQ, HEADS)
    hit_rank = jnp.take_along_axis(slot_rank, hits, axis=1)
    source = hit_rank * devices + hits
    owner_out = jnp.take(flat_out, source, axis=0)
    owner_lse = jnp.take(flat_lse, source, axis=0)
    every_lse = jnp.concatenate([prompt_lse[:, None], owner_lse], axis=1)
    highest = jnp.max(every_lse, axis=1)
    shares = jnp.exp(every_lse - highest[:, None])
    combined = shares[:, 0, :, :, None] * prompt_out + jnp.einsum(
        "rith,rithd->rthd", shares[:, 1:], owner_out, preferred_element_type=jnp.float32
    )
    result = combined / jnp.sum(shares, axis=1)[..., None]
    return result.astype(jnp.bfloat16).reshape(per_device, HEADS * HD)


def solution(mesh):
    in_specs = (
        P("groups"),
        P("groups", None),
        P("groups", None),
        P(("groups", "cache"), None),
        P(("groups", "cache"), None),
        P(("groups", "cache"), None),
        P(("groups", "cache"), None),
        P(("groups", "cache"), None),
    )
    out_specs = P(("groups", "cache"), None)
    return jax.shard_map(body, mesh=mesh, in_specs=in_specs, out_specs=out_specs, check_vma=False)
```

profile of v0, /device:TPU:9, one launch (start us, length us, event | category | flops | bytes accessed | tf_op | source)
XLA Modules:
  0.0 95.1 jit_solution(12392458391359597815)
XLA Ops:
  0.0 0.8 broadcast_compare_fusion.1
  0.8 0.1 multiply_reduce_fusion
  1.0 0.1 reshape.447
  1.1 1.1 %reshape.331 = bf16[16,4,2048]{2,1,0:T(4,128)(2,1)S(1)} reshape(bf16[64,2048]{1,0:T(8,128)(2,1)} %param.13) | data formatting | bytes 524288 | tf_op jit(solution)/shard_map/reshape | solution.py:114
  2.1 1.0 %gather_fusion.1 = bf16[32,4,2048]{2,1,0:T(4,128)(2,1)S(1)} fusion(bf16[16,4,2048]{2,1,0:T(4,128)(2,1)S(1)} %reshape.331, s32[1024]{0:T(1024)S(1)} %pad_clamp_fusion.1), kind=kCustom, calls=%fused_computation.1 | custom fusion | bytes 1048704 | tf_op jit(solution)/shard_map/jit(_take)/gather | solution.py:115
  3.1 0.0 copy-start.1
  3.1 0.0 copy-start.7
  3.1 0.3 copy.71
  3.4 0.1 broadcast_select_fusion
  3.6 1.2 %copy.72 = bf16[2,16,4,2048]{3,2,0,1:T(4,128)(2,1)} copy(bf16[2,16,4,2048]{3,1,0,2:T(8,128)(2,1)S(1)} %broadcast_select_fusion) | data formatting | bytes 1048576 | tf_op jit(solution)/shard_map/jit(_take)/select_n | solution.py:115
  4.8 6.6 %all-to-all-start = ((bf16[2,16,4,2048]{3,2,0,1:T(4,128)(2,1)}), bf16[2,16,4,2048]{3,2,0,1:T(4,128)(2,1)S(1)}, u32[]{:S(2)}, u32[]{:S(2)}) async-start(bf16[2,16,4,2048]{3,2,0,1:T(4,128)(2,1)} %copy.72), calls=%async_computation | async-start | bytes 1048576 | tf_op jit(solution)/shard_map/all_to_all | solution.py:116
  11.4 0.1 constant_dynamic-slice_fusion
  11.5 0.2 fusion.39
  11.7 0.2 select_reduce_fusion.1
  12.0 0.7 gather_fusion.4
  12.6 0.1 copy.90
  12.7 0.1 iota_add_fusion
  12.8 0.1 copy.67
  12.9 0.1 add.155
  13.0 0.1 broadcast_add_fusion
  13.0 0.1 copy.68
  13.1 23.2 %all_gather.6 = bf16[1024,128]{1,0:T(8,128)(2,1)S(1)} all-gather(bf16[64,128]{1,0:T(8,128)(2,1)S(1)} %copy-done.4), channel_id=1, replica_groups=mesh['groups'=2,'cache'=16] {'cache'}, dimensions={0}, use_global_device_ids=true | all-gather | bytes 278528 | tf_op jit(solution)/shard_map/all_gather | solution.py:88
  36.3 0.1 copy.70
  36.5 0.6 gather_fusion
  37.1 0.1 fusion.42
  37.2 0.4 fusion.43
  37.6 0.4 fusion.26
  38.0 0.1 compare_and_fusion
  38.1 0.0 all-to-all-done
  38.2 0.0 copy-start.5
  38.2 7.6 %while.20 = (s32[]{:T(128)}, bf16[2,16,4,2048]{3,1,2,0:T(8,128)(2,1)S(1)}, f32[2,16,4,16]{3,2,0,1:T(4,128)S(1)}, pred[2,1024]{1,0:T(4,128)(4,1)S(1)}, bf16[2,16,...) while((s32[]{:T(128)}, ...), condition=%wide.region_8.9_spmd, body=%wide.region_5.0_spmd.sunk | while | flops 550765568 | bytes 15906925 | solution.py:53
  38.2 0.1 dynamic-slice_bitcast_fusion.2
  38.3 0.2 squeeze.19
  38.5 0.8 fusion.57
  39.3 1.2 %fusion.58 = f32[64,16]{1,0:T(8,128)S(1)} fusion(f32[64,16,1024]{2,1,0:T(8,128)S(1)} %get-tuple-element.216, f32[1024]{0:T(1024)S(1)} %convert_element_type.76, f32[64,16]{1,0:T(8,128)S(1)} %get-tuple-element.217, pred[1024]{0:T(1024)(128)(4,1)S(1)} %dynamic-slice_reduce_fusion.2), kind=kLoop, calls=%fused_computation.8.clone.1 | loop fusion | flops 5241856 | bytes 4207616 | tf_op jit(solution)/shard_map/while/body/eval_jaxpr/while/body/eval_jaxpr/reduce_sum | solution.py:29
  40.5 1.1 %fusion.59 = bf16[64,16,128]{2,1,0:T(8,128)(2,1)S(1)} fusion(f32[64,16,1024]{2,1,0:T(8,128)S(1)} %get-tuple-element.216, f32[1024]{0:T(1024)S(1)} %convert_element_type.76, f32[64,16]{1,0:T(8,128)S(1)} %get-tuple-element.217, pred[1024]{0:T(1024)(128)(4,1)S(1)} %dynamic-slice_reduce_fusion.2, f32[64,16]{1,0:T(8,128)S(1)} %get-tuple-element.218, ...), kind=kOutput, calls=%fused_computation.13.clone.1 | convolution fusion | flops 273940480 | bytes 4789252 | tf_op jit(solution)/shard_map/while/body/eval_jaxpr/while/body/eval_jaxpr/thk,kd->thd/dot_general | solution.py:30
  41.7 0.1 broadcast_in_dim.205
  41.8 0.2 copy_dynamic-update-slice_fusion.2
  42.0 0.1 dynamic-slice_bitcast_fusion.2
  42.1 0.2 squeeze.19
  42.3 0.8 fusion.57
  43.1 1.2 %fusion.58 = f32[64,16]{1,0:T(8,128)S(1)} fusion(f32[64,16,1024]{2,1,0:T(8,128)S(1)} %get-tuple-element.216, f32[1024]{0:T(1024)S(1)} %convert_element_type.76, f32[64,16]{1,0:T(8,128)S(1)} %get-tuple-element.217, pred[1024]{0:T(1024)(128)(4,1)S(1)} %dynamic-slice_reduce_fusion.2), kind=kLoop, calls=%fused_computation.8.clone.1 | loop fusion | flops 5241856 | bytes 4207616 | tf_op jit(solution)/shard_map/while/body/eval_jaxpr/while/body/eval_jaxpr/reduce_sum | solution.py:29
  44.3 1.1 %fusion.59 = bf16[64,16,128]{2,1,0:T(8,128)(2,1)S(1)} fusion(f32[64,16,1024]{2,1,0:T(8,128)S(1)} %get-tuple-element.216, f32[1024]{0:T(1024)S(1)} %convert_element_type.76, f32[64,16]{1,0:T(8,128)S(1)} %get-tuple-element.217, pred[1024]{0:T(1024)(128)(4,1)S(1)} %dynamic-slice_reduce_fusion.2, f32[64,16]{1,0:T(8,128)S(1)} %get-tuple-element.218, ...), kind=kOutput, calls=%fused_computation.13.clone.1 | convolution fusion | flops 273940480 | bytes 4789252 | tf_op jit(solution)/shard_map/while/body/eval_jaxpr/while/body/eval_jaxpr/thk,kd->thd/dot_general | solution.py:30
  45.5 0.1 broadcast_in_dim.205
  45.6 0.2 copy_dynamic-update-slice_fusion.2
  45.7 0.7 reshape.490
  46.5 4.4 %all-to-all-start.1 = ((f32[16,1,128]{2,1,0:T(1,128)}), f32[16,1,128]{2,1,0:T(1,128)S(1)}, u32[]{:S(2)}, u32[]{:S(2)}) async-start(f32[16,1,128]{2,1,0:T(1,128)} %reshape.490), calls=%async_computation.1 | async-start | bytes 16384 | tf_op jit(solution)/shard_map/all_to_all | solution.py:124
  50.9 19.5 %all_gather.7 = bf16[1024,128]{1,0:T(8,128)(2,1)S(1)} all-gather(bf16[64,128]{1,0:T(8,128)(2,1)S(1)} %copy-done.5), channel_id=1, replica_groups=mesh['groups'=2,'cache'=16] {'cache'}, dimensions={0}, use_global_device_ids=true | all-gather | bytes 278528 | tf_op jit(solution)/shard_map/all_gather | solution.py:89
  70.4 0.1 copy.77
  70.5 1.2 %copy.79 = bf16[2,16,4,2048]{3,2,0,1:T(4,128)(2,1)} copy(bf16[2,16,4,2048]{3,1,2,0:T(8,128)(2,1)S(1)} %get-tuple-element.65) | data formatting | bytes 1048576 | tf_op jit(solution)/shard_map/convert_element_type | solution.py:122
  71.7 6.4 %all-to-all-start.2 = ((bf16[2,16,4,2048]{3,2,0,1:T(4,128)(2,1)}), bf16[2,16,4,2048]{3,2,0,1:T(4,128)(2,1)S(1)}, u32[]{:S(2)}, u32[]{:S(2)}) async-start(bf16[2,16,4,2048]{3,2,0,1:T(4,128)(2,1)} %copy.79), calls=%async_computation.2 | async-start | bytes 1048576 | tf_op jit(solution)/shard_map/all_to_all | solution.py:121
  78.2 0.5 broadcast.506
  78.7 0.7 reduce.10
  79.4 0.1 reshape.491
  79.5 0.6 gather_fusion.2
  80.1 0.1 bitcast_select_fusion
  80.2 0.1 fusion.32
  80.2 0.1 fusion.40
  80.3 12.0 %all-to-all-done.2 = bf16[2,16,4,2048]{3,2,0,1:T(4,128)(2,1)S(1)} async-done(((bf16[2,16,4,2048]{3,2,0,1:T(4,128)(2,1)}), bf16[2,16,4,2048]{3,2,0,1:T(4,128)(2,1)S(1)}, u32[]{:S(2)}, u32[]{:S(2)}) %all-to-all-start.2) | async-done | bytes 524320 | tf_op jit(solution)/shard_map/all_to_all | solution.py:121
  92.3 0.3 copy.80
  92.6 0.1 copy.94
  92.7 0.6 gather_fusion.3
  93.4 1.0 %fusion.25 = bf16[16,4,16,128]{3,2,1,0:T(8,128)(2,1)S(1)} fusion(bf16[16,64,128,1]{2,1,3,0:T(8,128)(2,1)S(1)} %bitcast.106, f32[16,4,16,64]{3,2,1,0:T(8,128)S(1)} %get-tuple-element.167, f32[16,4,16]{2,1,0:T(4,128)S(1)} %get-tuple-element.150, bf16[16,4,16,128]{3,2,1,0:T(8,128)(2,1)S(1)} %gather_fusion.3, f32[16,4,16]{2,1,0:T(4,128)S(1)} %get-tuple-element.161, ...), kind=kOutput, calls=%fused_computation.35 | convolution fusion | flops 101842944 | bytes 1085456 | tf_op jit(solution)/shard_map/rthk,rkd->rthd/dot_general | solution.py:110
  94.4 0.8 copy.98
  (45 shorter events, 0.4 us)
Async XLA Ops:
  0.0 36.5 %copy-start = (s32[16]{0:T(128)S(1)}, s32[16]{0:T(128)}, u32[]{:S(2)}) copy-start(s32[16]{0:T(128)} %param.10) | copy-start | bytes 196
  0.0 11.4 %copy-start.6 = (s32[16,1]{0,1:T(1,128)S(1)}, s32[16,1]{0,1:T(1,128)}, u32[]{:S(2)}) copy-start(s32[16,1]{0,1:T(1,128)} %param.11) | copy-start | bytes 196
  0.0 36.4 %copy-start.2 = (bf16[64,2048]{1,0:T(8,128)(2,1)S(1)}, bf16[64,2048]{1,0:T(8,128)(2,1)}, u32[]{:S(2)}) copy-start(bf16[64,2048]{1,0:T(8,128)(2,1)} %param.13) | copy-start | bytes 786436
  0.0 11.4 %copy-start.3 = (s32[16,16]{1,0:T(8,128)S(1)}, s32[16,16]{1,0:T(8,128)}, u32[]{:S(2)}) copy-start(s32[16,16]{1,0:T(8,128)} %param.12) | copy-start | bytes 3076
  0.0 13.1 %copy-start.4 = (bf16[64,128]{1,0:T(8,128)(2,1)S(1)}, bf16[64,128]{1,0:T(8,128)(2,1)}, u32[]{:S(2)}) copy-start(bf16[64,128]{1,0:T(8,128)(2,1)} %param.14) | copy-start | bytes 49156
  3.1 35.0 %copy-start.1 = (bf16[2048,128]{1,0:T(8,128)(2,1)S(1)}, bf16[2048,128]{1,0:T(8,128)(2,1)}, u32[]{:S(2)}) copy-start(bf16[2048,128]{1,0:T(8,128)(2,1)} %param.16) | copy-start | bytes 1572868
  3.1 35.0 %copy-start.7 = (bf16[2048,128]{1,0:T(8,128)(2,1)S(1)}, bf16[2048,128]{1,0:T(8,128)(2,1)}, u32[]{:S(2)}) copy-start(bf16[2048,128]{1,0:T(8,128)(2,1)} %param.17) | copy-start | bytes 1572868
  4.8 33.4 %all-to-all-start = ((bf16[2,16,4,2048]{3,2,0,1:T(4,128)(2,1)}), bf16[2,16,4,2048]{3,2,0,1:T(4,128)(2,1)S(1)}, u32[]{:S(2)}, u32[]{:S(2)}) async-start(bf16[2,16,4,2048]{3,2,0,1:T(4,128)(2,1)} %copy.72), calls=%async_computation | async-start | bytes 1048576 | tf_op jit(solution)/shard_map/all_to_all | solution.py:116
  38.2 12.7 %copy-start.5 = (bf16[64,128]{1,0:T(8,128)(2,1)S(1)}, bf16[64,128]{1,0:T(8,128)(2,1)}, u32[]{:S(2)}) copy-start(bf16[64,128]{1,0:T(8,128)(2,1)} %param.15) | copy-start | bytes 49156
  46.5 25.3 %all-to-all-start.1 = ((f32[16,1,128]{2,1,0:T(1,128)}), f32[16,1,128]{2,1,0:T(1,128)S(1)}, u32[]{:S(2)}, u32[]{:S(2)}) async-start(f32[16,1,128]{2,1,0:T(1,128)} %reshape.490), calls=%async_computation.1 | async-start | bytes 16384 | tf_op jit(solution)/shard_map/all_to_all | solution.py:124
  71.7 20.6 %all-to-all-start.2 = ((bf16[2,16,4,2048]{3,2,0,1:T(4,128)(2,1)}), bf16[2,16,4,2048]{3,2,0,1:T(4,128)(2,1)S(1)}, u32[]{:S(2)}, u32[]{:S(2)}) async-start(bf16[2,16,4,2048]{3,2,0,1:T(4,128)(2,1)} %copy.79), calls=%async_computation.2 | async-start | bytes 1048576 | tf_op jit(solution)/shard_map/all_to_all | solution.py:121
where the time goes:
time: 96.7 us; the launch traced here: 95.1 us
  blocking collectives  42.7 us (44%)
  starting transfers between devices  17.4 us (18%)
  waiting for transfers between devices  12 us (12%)
  local copies, waits for them, and re-layouts  11.6 us (12%)
  other arithmetic  5.57 us (6%)
  matrix products  5.26 us (5%)
    all_gather x1, blocking collectives, body(): key_piece = lax.all_gather(fresh_keys, 'cache', axis=0, tiled=True)  23.2 us
    all_gather x1, blocking collectives, body(): value_piece = lax.all_gather(fresh_values, 'cache', axis=0, tiled=True)  19.5 us
    all_to_all x1, waiting for transfers between devices, body(): lax.all_to_all(partial_out.astype(jnp.float32), 'cache', split_axis=1, co...  12 us
    all_to_all x1, starting transfers between devices, body(): lax.all_to_all(outgoing, 'cache', split_axis=1, concat_axis=1, tiled=True)  6.61 us
    all_to_all x1, starting transfers between devices, body(): lax.all_to_all(partial_out.astype(jnp.float32), 'cache', split_axis=1, co...  6.44 us
    all_to_all x1, starting transfers between devices, body(): lax.all_to_all(partial_lse, 'cache', split_axis=1, concat_axis=1, tiled=T...  4.39 us
    reduce_sum x2, other arithmetic, owner_block(): totals = jnp.maximum(jnp.sum(weights, axis=2), 1.0)  2.34 us
    dot_general x2, matrix products, owner_block(): jnp.einsum('thk,kd->thd', weights.astype(jnp.bfloat16), page_values, pref...  2.27 us
  transfers between devices with their start and end apart: 3, of which 1 were waited for; matrix products, arithmetic and copies ran while one was open for 7% of the time, Pallas kernels for 0%

commit v1 on v0

v1 whole, which is shorter than its diff:
```python
import functools
import math

import jax
import jax.numpy as jnp
from jax import lax
from jax.experimental import pallas as pl
from jax.experimental.pallas import tpu as pltpu
from jax.sharding import PartitionSpec as P

HEADS = 16
HD = 128
PAGE = 128
CAP = 2
REQUESTS = 16
TOK = 4
PAGES_DEV = 16
REGION = PAGES_DEV // CAP * PAGE
PER_DEV = REQUESTS * TOK
PLANE = 4
ROWS = PLANE * TOK * HEADS
MESH = pl.DeviceIdType.MESH
FLOOR = -1e30
EXP2_SCALE = HD**-0.5 * math.log2(math.e)


def flip(a, b, size):
    out, bit = 0, 1
    while bit < size:
        out = out + ((a // bit + b // bit) % 2) * bit
        bit *= 2
    return out


def attend(q, k, v, visible):
    s = lax.dot_general(q, k, (((1,), (1,)), ((), ())), preferred_element_type=jnp.float32)
    s = jnp.where(visible, s, FLOOR)
    m = jnp.max(s, axis=1, keepdims=True)
    p = jnp.exp2((s - m) * EXP2_SCALE).astype(jnp.bfloat16)
    v1 = jnp.concatenate([v, jnp.ones_like(v)], axis=1)
    o = jnp.dot(p, v1, preferred_element_type=jnp.float32)
    return m, o


def head_lanes(x, units):
    x = x.reshape(units, HEADS, HD)
    head = lax.broadcasted_iota(jnp.int32, (units, HEADS, HD), 1)
    lane = lax.broadcasted_iota(jnp.int32, (units, HEADS, HD), 2)
    return jnp.sum(jnp.where(head == lane, x, 0.0), axis=1)


def head_rows(x, units):
    head = lax.broadcasted_iota(jnp.int32, (units, HEADS, HD), 1)
    lane = lax.broadcasted_iota(jnp.int32, (units, HEADS, HD), 2)
    wide = jnp.broadcast_to(x[:, None, :], (units, HEADS, HD))
    return jnp.sum(jnp.where(head == lane, wide, 0.0), axis=2, keepdims=True)


def kernel(n, hit_count, dims, prefix, hits, span, qx, fk, fv, ck, cv, out,
           send, arrived, ret, back, lret, lback, kv, kc, vc, pout, plse, comb, lcomb,
           qs, qr, rs, rr, ls, lr, s1s, s1r, s2s, s2r, s3s, s3r, loc):
    me = lax.axis_index("cache")
    zs, ys = dims
    planes = n // PLANE
    core = me % 2
    y = (me // 2) % ys
    z = me // (2 * ys)
    my_plane = me // PLANE

    loads = [
        pltpu.make_async_copy(fk, kv.at[z, y, core, 0], loc.at[0]),
        pltpu.make_async_copy(fv, kv.at[z, y, core, 1], loc.at[1]),
        pltpu.make_async_copy(ck, kc, loc.at[2]),
        pltpu.make_async_copy(cv, vc, loc.at[3]),
    ]
    for load in loads:
        load.start()

    barrier = pltpu.get_barrier_semaphore()

    @pl.loop(1, n)
    def _(k):
        pl.semaphore_signal(barrier, inc=1, device_id={"cache": (me + k) % n}, device_id_type=MESH)

    def named_by(d):
        first = jnp.int32(REQUESTS - 1)
        last = jnp.int32(0)
        for r in range(REQUESTS):
            for i in range(hit_count):
                here = hits[r, i] == d
                first = jnp.where(here, jnp.minimum(first, r), first)
                last = jnp.where(here, r, last)
        return first, last

    @pl.loop(0, n)
    def _(d):
        first, last = named_by(d)
        send[d, 0] = qx[first]
        send[d, 1] = qx[last]

    pl.semaphore_wait(barrier, n - 1)
    loads[0].wait()
    loads[1].wait()

    def kv1(dz, at_z):
        return pltpu.make_async_remote_copy(
            src_ref=kv.at[at_z, y, core], dst_ref=kv.at[at_z, y, core],
            send_sem=s1s.at[dz], recv_sem=s1r.at[dz],
            device_id={"cache": (((z + dz) % zs) * ys + y) * 2 + core}, device_id_type=MESH)

    def kv2(dy, at_y):
        return pltpu.make_async_remote_copy(
            src_ref=kv.at[:, at_y, core], dst_ref=kv.at[:, at_y, core],
            send_sem=s2s.at[dy], recv_sem=s2r.at[dy],
            device_id={"cache": (z * ys + (y + dy) % ys) * 2 + core}, device_id_type=MESH)

    def kv3(at_core):
        return pltpu.make_async_remote_copy(
            src_ref=kv.at[:, :, at_core], dst_ref=kv.at[:, :, at_core],
            send_sem=s3s.at[0], recv_sem=s3r.at[0],
            device_id={"cache": (z * ys + y) * 2 + 1 - core}, device_id_type=MESH)

    for dz in range(1, zs):
        kv1(dz, z).start()

    def query_copy(to, frm):
        return pltpu.make_async_remote_copy(
            src_ref=send.at[to], dst_ref=arrived.at[frm], send_sem=qs.at[to], recv_sem=qr.at[frm],
            device_id={"cache": to}, device_id_type=MESH)

    def out_copy(to, frm):
        return pltpu.make_async_remote_copy(
            src_ref=ret.at[to], dst_ref=back.at[frm], send_sem=rs.at[to], recv_sem=rr.at[frm],
            device_id={"cache": to}, device_id_type=MESH)

    def lse_copy(to, frm):
        return pltpu.make_async_remote_copy(
            src_ref=lret.at[to], dst_ref=lback.at[frm], send_sem=ls.at[to], recv_sem=lr.at[frm],
            device_id={"cache": to}, device_id_type=MESH)

    def peers(j, act):
        base = flip(my_plane, j, planes) * PLANE

        @pl.loop(0, PLANE)
        def _(k):
            d = base + (me + k) % PLANE

            @pl.when(d != me)
            def _():
                act(d)

    @pl.loop(0, planes)
    def _(i):
        peers((planes // 2 + i) % planes, lambda d: query_copy(d, me).start())

    arrived[me] = send[me]
    loads[2].wait()
    loads[3].wait()

    limits = []
    for request in named_by(me):
        place = jnp.int32(0)
        for i in range(hit_count):
            place = jnp.where(hits[request, i] == me, i, place)
        limits.append(prefix[request] - place * REGION)
    spot = lax.broadcasted_iota(jnp.int32, (1, REGION), 1)

    def serve(j):
        peers(j, lambda d: query_copy(d, d).wait_recv())
        base = flip(my_plane, j, planes) * PLANE

        for slot in range(CAP):
            q = arrived[pl.ds(base, PLANE), slot].reshape(ROWS, HD)
            part = pl.ds(slot * REGION, REGION)
            m, o = attend(q, kc[part], vc[part], spot < limits[slot])
            total = jnp.maximum(o[:, HD:], 1.0)
            lse = m * EXP2_SCALE + jnp.log2(total)
            lse = jnp.where(limits[slot] > 0, lse, FLOOR)
            result = (o[:, :HD] / total).astype(jnp.bfloat16)
            ret[pl.ds(base, PLANE), slot] = result.reshape(PLANE, TOK, HEADS, HD)
            lanes = head_lanes(lse, PLANE * TOK)
            for k in range(PLANE):
                lret[base + k, slot] = lanes[k * TOK:(k + 1) * TOK]

        def go(d):
            out_copy(d, me).start()
            lse_copy(d, me).start()

        peers(j, go)

    pl.loop(0, 1)(serve)
    for dz in range(1, zs):
        kv1(dz, (z + zs - dz) % zs).wait_recv()
    for dy in range(1, ys):
        kv2(dy, y).start()
    pl.loop(1, 2)(serve)
    for dy in range(1, ys):
        kv2(dy, (y + ys - dy) % ys).wait_recv()
    kv3(core).start()
    pl.loop(2, planes)(serve)
    back[me] = ret[me]
    lback[me] = lret[me]
    kv3(1 - core).wait_recv()

    span_f = span[...].astype(jnp.float32)
    mine = jnp.sum(
        jnp.where(lax.broadcasted_iota(jnp.int32, span_f.shape, 1) == me, span_f, 0.0),
        axis=1, keepdims=True)
    order = jnp.clip(span_f - mine, -1.0, 1.0).astype(jnp.bfloat16)
    group = 16
    keys = group * PER_DEV
    zgroup = group // (2 * ys)
    chunks = n // group
    key_lane = lax.broadcasted_iota(jnp.int32, (REQUESTS, keys), 1)
    key_row = lax.broadcasted_iota(jnp.int32, (REQUESTS, keys), 0)

    def ranks(chunk):
        lane = lax.broadcasted_iota(jnp.int32, (n, keys), 1)
        dev = lax.broadcasted_iota(jnp.int32, (n, keys), 0)
        pick = jnp.where(lane // PER_DEV + chunk * group == dev, 1.0, 0.0).astype(jnp.bfloat16)
        step = jnp.dot(order, pick, preferred_element_type=jnp.float32)
        spot_rank = step * TOK + (key_lane % TOK).astype(jnp.float32)
        same = (key_lane // TOK) % REQUESTS == key_row
        return jnp.where(same, spot_rank, 100.0).astype(jnp.bfloat16)

    def kv_rows(chunk, which):
        if chunks == 1:
            return kv[:, :, :, which].reshape(keys, HD)
        flat = kv.at[:, :, :, which]
        per_z = (2 * ys) // group
        if per_z:
            got = flat[chunk // per_z, pl.ds((chunk % per_z) * (group // 2), group // 2)]
        else:
            got = flat[pl.ds(chunk * zgroup, zgroup)]
        return got.reshape(keys, HD)

    def prompt_part(c, chunk, rank):
        q = qx_rows(c)
        row = lax.broadcasted_iota(jnp.int32, (ROWS, REQUESTS), 0)
        req = lax.broadcasted_iota(jnp.int32, (ROWS, REQUESTS), 1)
        spread = jnp.where(row // (TOK * HEADS) + c * (ROWS // (TOK * HEADS)) == req, 1.0, 0.0)
        ranked = jnp.dot(spread.astype(jnp.bfloat16), rank, preferred_element_type=jnp.float32)
        token = (lax.broadcasted_iota(jnp.int32, (ROWS, 1), 0) // HEADS) % TOK
        return attend(q, kv_rows(chunk, 0), kv_rows(chunk, 1), ranked <= token.astype(jnp.float32))

    reqs = ROWS // (TOK * HEADS)

    def qx_rows(c):
        return qx[pl.ds(c * reqs, reqs)].reshape(ROWS, HD)

    rank0 = ranks(0) if chunks == 1 else None

    @pl.loop(0, REQUESTS // reqs)
    def _(c):
        if chunks == 1:
            m, o = prompt_part(c, 0, rank0)
        else:
            def more(chunk, carry):
                m0, o0 = carry
                m1, o1 = prompt_part(c, chunk, ranks(chunk))
                m2 = jnp.maximum(m0, m1)
                return m2, (o0 * jnp.exp2((m0 - m2) * EXP2_SCALE)
                            + o1 * jnp.exp2((m1 - m2) * EXP2_SCALE))
            m, o = lax.fori_loop(0, chunks, more, (
                jnp.full((ROWS, 1), FLOOR, jnp.float32), jnp.zeros((ROWS, 2 * HD), jnp.float32)))
        total = o[:, HD:]
        pout[pl.ds(c * reqs, reqs)] = (o[:, :HD] / total).reshape(reqs, TOK, HEADS, HD)
        lanes = head_lanes(m * EXP2_SCALE + jnp.log2(total), reqs * TOK)
        plse[pl.ds(pl.multiple_of(c * reqs * TOK, reqs * TOK), reqs * TOK)] = lanes

    def finish(d):
        out_copy(d, d).wait_recv()
        lse_copy(d, d).wait_recv()

    pl.loop(0, planes)(lambda j: peers(j, finish))

    for i in range(hit_count):
        for r in range(REQUESTS):
            owner = hits[r, i]
            rank = jnp.int32(0)
            for r2 in range(r):
                for i2 in range(hit_count):
                    rank = jnp.where(hits[r2, i2] == owner, rank + 1, rank)
            rank = jnp.minimum(rank, CAP - 1)
            comb[i, r] = back[owner, rank]
            lcomb[i, r * TOK:(r + 1) * TOK] = lback[owner, rank]

    top = plse[...]
    for i in range(hit_count):
        top = jnp.maximum(top, lcomb[i])
    share = jnp.exp2(plse[...] - top)
    shares = [jnp.exp2(lcomb[i] - top) for i in range(hit_count)]
    scale = 1.0 / functools.reduce(jnp.add, shares, share)
    whole = (PER_DEV, HEADS, HD)
    mixed = head_rows(share * scale, PER_DEV) * pout[...].reshape(whole)
    for i in range(hit_count):
        mixed = mixed + head_rows(shares[i] * scale, PER_DEV) * comb[i].reshape(whole).astype(jnp.float32)
    out[...] = mixed.astype(jnp.bfloat16)

    def drained(d):
        query_copy(d, me).wait_send()
        out_copy(d, me).wait_send()
        lse_copy(d, me).wait_send()

    pl.loop(0, planes)(lambda j: peers(j, drained))
    for dz in range(1, zs):
        kv1(dz, z).wait_send()
    for dy in range(1, ys):
        kv2(dy, y).wait_send()
    kv3(core).wait_send()


def solution(mesh):
    n = mesh.shape["cache"]
    rest = n // 2
    zs = 2 ** ((int(math.log2(rest)) + 1) // 2)
    dims = (zs, rest // zs)

    def body(prefix_len, hits, span_block, queries, fresh_keys, fresh_values, cache_keys, cache_values):
        hit_count = hits.shape[1]
        units = queries.reshape(REQUESTS, TOK, HEADS, HD)
        vmem = pl.BlockSpec(memory_space=pltpu.VMEM)
        smem = pl.BlockSpec(memory_space=pltpu.SMEM)
        hbm = pl.BlockSpec(memory_space=pltpu.HBM)
        bf16, f32 = jnp.bfloat16, jnp.float32
        dma = pltpu.SemaphoreType.DMA
        block = (n, CAP, TOK, HEADS, HD)
        result = pl.pallas_call(
            functools.partial(kernel, n, hit_count, dims),
            out_shape=jax.ShapeDtypeStruct((PER_DEV, HEADS, HD), bf16),
            in_specs=[smem, smem, vmem, vmem, hbm, hbm, hbm, hbm],
            out_specs=vmem,
            scratch_shapes=[
                pltpu.VMEM(block, bf16), pltpu.VMEM(block, bf16),
                pltpu.VMEM(block, bf16), pltpu.VMEM(block, bf16),
                pltpu.VMEM((n, CAP, TOK, HD), f32), pltpu.VMEM((n, CAP, TOK, HD), f32),
                pltpu.VMEM(dims + (2, 2, PER_DEV, HD), bf16),
                pltpu.VMEM((CAP * REGION, HD), bf16), pltpu.VMEM((CAP * REGION, HD), bf16),
                pltpu.VMEM((REQUESTS, TOK, HEADS, HD), f32), pltpu.VMEM((PER_DEV, HD), f32),
                pltpu.VMEM((hit_count, REQUESTS, TOK, HEADS, HD), bf16),
                pltpu.VMEM((hit_count, PER_DEV, HD), f32),
            ] + [dma((n,))] * 6 + [dma((dims[0],))] * 2 + [dma((dims[1],))] * 2 + [dma((1,))] * 2 + [dma((4,))],
            compiler_params=pltpu.CompilerParams(
                collective_id=0, has_side_effects=True, vmem_limit_bytes=48 << 20),
        )(prefix_len, hits, span_block, units, fresh_keys, fresh_values, cache_keys, cache_values)
        return result.reshape(PER_DEV, HEADS * HD)

    in_specs = (
        P("groups"), P("groups", None), P("groups", None),
        P(("groups", "cache"), None), P(("groups", "cache"), None), P(("groups", "cache"), None),
        P(("groups", "cache"), None), P(("groups", "cache"), None),
    )
    return jax.shard_map(body, mesh=mesh, in_specs=in_specs,
                         out_specs=P(("groups", "cache"), None), check_vma=False)
```

time: 96.7 us -> 42.6 us (0.44); the launches traced: 95.1 us -> 42.2 us
  blocking collectives: 42.7 us -> 0 us
  Pallas kernels: 0 us -> 36.5 us
  starting transfers between devices: 17.4 us -> 0 us
  waiting for transfers between devices: 12 us -> 0 us
  local copies, waits for them, and re-layouts: 11.6 us -> 5.67 us
  other arithmetic: 5.57 us -> 0 us
  matrix products: 5.26 us -> 0 us
    all_gather x2 -> x0, blocking collectives: 42.7 us -> none  [the longest x1 23.2 us: body(): key_piece = lax.all_gather(fresh_keys, 'cache', axis=0, tiled=True)]
    pallas_call x0 -> x1, Pallas kernels: none -> 36.5 us  [body(): pl.pallas_call(functools.partial(kernel, n, hit_count, dims), out_shape=j...]
    all_to_all x3 -> x0, starting transfers between devices: 17.4 us -> none  [the longest x1 6.61 us: body(): lax.all_to_all(outgoing, 'cache', split_axis=1, concat_axis=1, tiled=True)]
    all_to_all x3 -> x0, waiting for transfers between devices: 12 us -> none  [the longest x1 12 us: body(): lax.all_to_all(partial_out.astype(jnp.float32), 'cache', split_axis=1, co...]
    dot_general x6 -> x0, matrix products: 5.26 us -> none  [the longest x2 2.27 us: owner_block(): jnp.einsum('thk,kd->thd', weights.astype(jnp.bfloat16), page_values, pref...]
    unnamed x23 -> x15, local copies, waits for them, and re-layouts: 1.85 us -> 5.67 us
    gather x6 -> x0, local copies, waits for them, and re-layouts: 3.8 us -> none  [the longest x2 1.29 us: body(): outgoing = jnp.take(units, send_request, axis=0)]
    reduce_sum x6 -> x0, other arithmetic: 2.96 us -> none  [the longest x2 2.34 us: owner_block(): totals = jnp.maximum(jnp.sum(weights, axis=2), 1.0)]
  transfers between devices with their start and end apart: 3 -> 0, of which waited for: 1 -> 0; matrix products, arithmetic and copies ran while one was open for 7% -> 0% of each run, Pallas kernels for 0% -> 0%
where the time goes in v1:
time: 42.6 us; the launch traced here: 42.2 us
  Pallas kernels  36.5 us (86%)
  local copies, waits for them, and re-layouts  5.67 us (13%)
    pallas_call x1, Pallas kernels, body(): pl.pallas_call(functools.partial(kernel, n, hit_count, dims), out_shape=j...  36.5 us
    unnamed x15, local copies, waits for them, and re-layouts  5.67 us

profile of v1, /device:TPU:9, one launch (start us, length us, event | category | flops | bytes accessed | tf_op | source)
XLA Modules:
  0.0 42.2 jit_solution(4350755577993914381)
XLA Ops:
  0.0 0.0 copy-start
  0.0 0.8 %copy.9.hits = s32[16,1]{1,0:T(8,128)S(1)} copy(s32[16,1]{0,1:T(1,128)} %param.9) | data formatting | bytes 128 | tf_op args[1]
  0.8 0.0 copy-start.4
  0.8 1.0 %copy.10 = bf16[8,8,16,128]{3,2,1,0:T(8,128)(2,1)S(1)} copy(bf16[8,8,16,128]{3,1,2,0:T(8,128)(2,1)} %bitcast.9) | data formatting | bytes 524288
  1.8 0.0 copy-start.5
  1.8 0.0 copy-done
  1.8 0.0 copy-done.4
  1.8 0.6 %copy-done.5 = s32[16]{0:T(128)S(1)} copy-done((s32[16]{0:T(128)S(1)}, s32[16]{0:T(128)}, u32[]{:S(2)}) %copy-start.5) | copy-done | bytes 88
  2.5 0.0 copy-start.1
  2.5 1.0 %copy-done.1 = bf16[2048,128]{1,0:T(8,128)(2,1)S(1)} copy-done((bf16[2048,128]{1,0:T(8,128)(2,1)S(1)}, bf16[2048,128]{1,0:T(8,128)(2,1)}, u32[]{:S(2)}) %copy-start.1) | copy-done | bytes 524312
  3.5 0.0 copy-start.2
  3.5 0.7 %copy-done.2 = bf16[64,128]{1,0:T(8,128)(2,1)S(1)} copy-done((bf16[64,128]{1,0:T(8,128)(2,1)S(1)}, bf16[64,128]{1,0:T(8,128)(2,1)}, u32[]{:S(2)}) %copy-start.2) | copy-done | bytes 16408
  4.2 0.0 copy-start.3
  4.2 0.7 %copy-done.3 = bf16[64,128]{1,0:T(8,128)(2,1)S(1)} copy-done((bf16[64,128]{1,0:T(8,128)(2,1)S(1)}, bf16[64,128]{1,0:T(8,128)(2,1)}, u32[]{:S(2)}) %copy-start.3) | copy-done | bytes 16408
  4.9 36.5 %shard_map.82 = bf16[64,16,128]{2,1,0:T(8,128)(2,1)S(1)} custom-call(s32[16]{0:T(128)S(1)} %copy-done.5, s32[16,1]{1,0:T(8,128)S(1)} %copy.9.hits, s32[16,16]{1,0:T(8,128)S(1)} %copy-done.4, bf16[16,4,16,128]{3,2,1,0:T(8,128)(2,1)S(1)} %bitcast.8, bf16[64,128]{1,0:T(8,128)(2,1)S(1)} %copy-done.2, bf16[64,128]{1,0:T(8,128)(2,1)S(1)} %copy-done.3, ...), custom_call_target="tpu_custom_call" | custom-call | tf_op jit(solution)/shard_map/pallas_call | solution.py:328
  41.5 0.8 %copy.13 = bf16[8,8,16,128]{3,1,2,0:T(8,128)(2,1)} copy(bf16[8,8,16,128]{3,2,1,0:T(8,128)(2,1)S(1)} %bitcast.7) | data formatting | bytes 524288
Async XLA Ops:
  0.0 1.8 %copy-start = (bf16[2048,128]{1,0:T(8,128)(2,1)S(1)}, bf16[2048,128]{1,0:T(8,128)(2,1)}, u32[]{:S(2)}) copy-start(bf16[2048,128]{1,0:T(8,128)(2,1)} %ck.1) | copy-start | bytes 1572868
  0.8 1.0 %copy-start.4 = (s32[16,16]{1,0:T(8,128)S(1)}, s32[16,16]{1,0:T(8,128)}, u32[]{:S(2)}) copy-start(s32[16,16]{1,0:T(8,128)} %span.1) | copy-start | bytes 3076
  1.8 0.7 %copy-start.5 = (s32[16]{0:T(128)S(1)}, s32[16]{0:T(128)}, u32[]{:S(2)}) copy-start(s32[16]{0:T(128)} %prefix.1) | copy-start | bytes 196
  2.5 1.0 %copy-start.1 = (bf16[2048,128]{1,0:T(8,128)(2,1)S(1)}, bf16[2048,128]{1,0:T(8,128)(2,1)}, u32[]{:S(2)}) copy-start(bf16[2048,128]{1,0:T(8,128)(2,1)} %cv.1) | copy-start | bytes 1572868
  3.5 0.7 %copy-start.2 = (bf16[64,128]{1,0:T(8,128)(2,1)S(1)}, bf16[64,128]{1,0:T(8,128)(2,1)}, u32[]{:S(2)}) copy-start(bf16[64,128]{1,0:T(8,128)(2,1)} %fk.1) | copy-start | bytes 49156
  4.2 0.7 %copy-start.3 = (bf16[64,128]{1,0:T(8,128)(2,1)S(1)}, bf16[64,128]{1,0:T(8,128)(2,1)}, u32[]{:S(2)}) copy-start(bf16[64,128]{1,0:T(8,128)(2,1)} %fv.1) | copy-start | bytes 49156

commit v2 on v1

v2 whole, which is shorter than its diff:
```python
import functools
import math

import jax
import jax.numpy as jnp
from jax import lax
from jax.experimental import pallas as pl
from jax.experimental.pallas import tpu as pltpu
from jax.sharding import PartitionSpec as P

HEADS = 16
HD = 128
PAGE = 128
CAP = 2
REQUESTS = 16
TOK = 4
PAGES_DEV = 16
REGION = PAGES_DEV // CAP * PAGE
PER_DEV = REQUESTS * TOK
PLANE = 4
ROWS = PLANE * TOK * HEADS
MESH = pl.DeviceIdType.MESH
FLOOR = -1e30
EXP2_SCALE = HD**-0.5 * math.log2(math.e)


def flip(a, b, size):
    out, bit = 0, 1
    while bit < size:
        out = out + ((a // bit + b // bit) % 2) * bit
        bit *= 2
    return out


def attend(q, k, v, visible):
    s = lax.dot_general(q, k, (((1,), (1,)), ((), ())), preferred_element_type=jnp.float32)
    s = jnp.where(visible, s, FLOOR)
    m = jnp.max(s, axis=1, keepdims=True)
    p = jnp.exp2((s - m) * EXP2_SCALE).astype(jnp.bfloat16)
    v1 = jnp.concatenate([v, jnp.ones_like(v)], axis=1)
    o = jnp.dot(p, v1, preferred_element_type=jnp.float32)
    return m, o


def head_lanes(x, units, first):
    row = lax.broadcasted_iota(jnp.int32, (units, TOK * HEADS, HD), 1)
    lane = lax.broadcasted_iota(jnp.int32, (units, TOK * HEADS, HD), 2)
    wide = x.reshape(units, TOK * HEADS, HD)
    return jnp.sum(jnp.where(row + first == lane, wide, 0.0), axis=1)


def head_rows(x, units):
    row = lax.broadcasted_iota(jnp.int32, (units, TOK * HEADS, HD), 1)
    lane = lax.broadcasted_iota(jnp.int32, (units, TOK * HEADS, HD), 2)
    wide = jnp.broadcast_to(x[:, None, :], (units, TOK * HEADS, HD))
    return jnp.sum(jnp.where(row == lane, wide, 0.0), axis=2, keepdims=True)


def mirrored(a, size):
    out, bit = 0, 1
    while bit < size:
        out = out + ((a // bit) % 2) * (size // (2 * bit))
        bit *= 2
    return out


def kernel(n, hit_count, prefix, hits, span, queries, fk, fv, ck, cv, out,
           qin, qx, send, arrived, ret, back, lret, lback, kv, kc, vc, pout, plse, comb, lcomb,
           qs, qr, rs, rr, ls, lr, s1s, s1r, loc):
    me = lax.axis_index("cache")
    planes = n // PLANE
    stages = int(math.log2(n))
    spot_me = mirrored(me, n)
    my_plane = me // PLANE

    loads = [
        pltpu.make_async_copy(queries, qin, loc.at[4]),
        pltpu.make_async_copy(fk, kv.at[spot_me, 0], loc.at[0]),
        pltpu.make_async_copy(fv, kv.at[spot_me, 1], loc.at[1]),
        pltpu.make_async_copy(ck, kc, loc.at[2]),
        pltpu.make_async_copy(cv, vc, loc.at[3]),
    ]
    for load in loads:
        load.start()

    barrier = pltpu.get_barrier_semaphore()

    @pl.loop(1, n)
    def _(k):
        pl.semaphore_signal(barrier, inc=1, device_id={"cache": (me + k) % n}, device_id_type=MESH)

    def named_by(d):
        first = jnp.int32(REQUESTS - 1)
        last = jnp.int32(0)
        for r in range(REQUESTS):
            for i in range(hit_count):
                here = hits[r * hit_count + i] == d
                first = jnp.where(here, jnp.minimum(first, r), first)
                last = jnp.where(here, r, last)
        return first, last

    loads[0].wait()
    qx[...] = qin[...].reshape(REQUESTS, TOK, HEADS, HD)

    @pl.loop(0, n)
    def _(d):
        first, last = named_by(d)
        send[d, 0] = qx[first]
        send[d, 1] = qx[last]

    pl.semaphore_wait(barrier, n - 1)
    loads[1].wait()
    loads[2].wait()

    def kv_copy(t, mine=True):
        size = 2**t
        start = (spot_me // size) * size
        if not mine:
            start = flip(spot_me // size, 1, n // size) * size
        block = kv.at[pl.ds(start, size)]
        return pltpu.make_async_remote_copy(
            src_ref=block, dst_ref=block, send_sem=s1s.at[t], recv_sem=s1r.at[t],
            device_id={"cache": flip(me, n // (2 * size), n)}, device_id_type=MESH)

    kv_copy(0).start()

    def query_copy(to, frm):
        return pltpu.make_async_remote_copy(
            src_ref=send.at[to], dst_ref=arrived.at[frm], send_sem=qs.at[to], recv_sem=qr.at[frm],
            device_id={"cache": to}, device_id_type=MESH)

    def out_copy(to, frm):
        return pltpu.make_async_remote_copy(
            src_ref=ret.at[to], dst_ref=back.at[frm], send_sem=rs.at[to], recv_sem=rr.at[frm],
            device_id={"cache": to}, device_id_type=MESH)

    def lse_copy(to, frm):
        return pltpu.make_async_remote_copy(
            src_ref=lret.at[to], dst_ref=lback.at[frm], send_sem=ls.at[to], recv_sem=lr.at[frm],
            device_id={"cache": to}, device_id_type=MESH)

    def peers(j, act):
        base = flip(my_plane, j, planes) * PLANE

        @pl.loop(0, PLANE)
        def _(k):
            d = base + (me + k) % PLANE

            @pl.when(d != me)
            def _():
                act(d)

    @pl.loop(0, planes)
    def _(i):
        peers(i, lambda d: query_copy(d, me).start())

    arrived[me] = send[me]
    loads[3].wait()
    loads[4].wait()

    limits = []
    for request in named_by(me):
        place = jnp.int32(0)
        for i in range(hit_count):
            place = jnp.where(hits[request * hit_count + i] == me, i, place)
        limits.append(prefix[request] - place * REGION)
    spot = lax.broadcasted_iota(jnp.int32, (1, REGION), 1)

    def serve(j):
        peers(j, lambda d: query_copy(d, d).wait_recv())
        base = flip(my_plane, j, planes) * PLANE
        lanes = jnp.zeros((PLANE, HD), jnp.float32)

        for slot in range(CAP):
            q = arrived[pl.ds(base, PLANE), slot].reshape(ROWS, HD)
            part = pl.ds(slot * REGION, REGION)
            m, o = attend(q, kc[part], vc[part], spot < limits[slot])
            total = jnp.maximum(o[:, HD:], 1.0)
            lse = m * EXP2_SCALE + jnp.log2(total)
            lse = jnp.where(limits[slot] > 0, lse, FLOOR)
            result = (o[:, :HD] / total).astype(jnp.bfloat16)
            ret[pl.ds(base, PLANE), slot] = result.reshape(PLANE, TOK, HEADS, HD)
            lanes = lanes + head_lanes(lse, PLANE, slot * TOK * HEADS)
        for k in range(PLANE):
            lret[base + k] = lanes[k:k + 1]

        def go(d):
            out_copy(d, me).start()
            lse_copy(d, me).start()

        peers(j, go)

        for t in range(stages - 1):
            @pl.when(j == t)
            def _():
                kv_copy(t, mine=False).wait_recv()
                kv_copy(t + 1).start()

    pl.loop(0, planes)(serve)
    back[me] = ret[me]
    lback[me] = lret[me]
    kv_copy(stages - 1, mine=False).wait_recv()

    span_f = span[...].astype(jnp.float32)
    mine = jnp.sum(
        jnp.where(lax.broadcasted_iota(jnp.int32, span_f.shape, 1) == me, span_f, 0.0),
        axis=1, keepdims=True)
    order = jnp.clip(span_f - mine, -1.0, 1.0).astype(jnp.bfloat16)
    group = 16
    keys = group * PER_DEV
    chunks = n // group
    key_lane = lax.broadcasted_iota(jnp.int32, (REQUESTS, keys), 1)
    key_row = lax.broadcasted_iota(jnp.int32, (REQUESTS, keys), 0)

    def ranks(chunk):
        lane = lax.broadcasted_iota(jnp.int32, (n, keys), 1)
        dev = lax.broadcasted_iota(jnp.int32, (n, keys), 0)
        pick = jnp.where(mirrored(lane // PER_DEV + chunk * group, n) == dev, 1.0, 0.0).astype(jnp.bfloat16)
        step = jnp.dot(order, pick, preferred_element_type=jnp.float32)
        spot_rank = step * TOK + (key_lane % TOK).astype(jnp.float32)
        same = (key_lane // TOK) % REQUESTS == key_row
        return jnp.where(same, spot_rank, 100.0).astype(jnp.bfloat16)

    def kv_rows(chunk, which):
        return kv[pl.ds(chunk * group, group), which].reshape(keys, HD)

    def prompt_part(c, chunk, rank):
        q = qx_rows(c)
        row = lax.broadcasted_iota(jnp.int32, (ROWS, REQUESTS), 0)
        req = lax.broadcasted_iota(jnp.int32, (ROWS, REQUESTS), 1)
        spread = jnp.where(row // (TOK * HEADS) + c * (ROWS // (TOK * HEADS)) == req, 1.0, 0.0)
        ranked = jnp.dot(spread.astype(jnp.bfloat16), rank, preferred_element_type=jnp.float32)
        token = (lax.broadcasted_iota(jnp.int32, (ROWS, 1), 0) // HEADS) % TOK
        return attend(q, kv_rows(chunk, 0), kv_rows(chunk, 1), ranked <= token.astype(jnp.float32))

    reqs = ROWS // (TOK * HEADS)

    def qx_rows(c):
        return qx[pl.ds(c * reqs, reqs)].reshape(ROWS, HD)

    rank0 = ranks(0) if chunks == 1 else None

    @pl.loop(0, REQUESTS // reqs)
    def _(c):
        if chunks == 1:
            m, o = prompt_part(c, 0, rank0)
        else:
            def more(chunk, carry):
                m0, o0 = carry
                m1, o1 = prompt_part(c, chunk, ranks(chunk))
                m2 = jnp.maximum(m0, m1)
                return m2, (o0 * jnp.exp2((m0 - m2) * EXP2_SCALE)
                            + o1 * jnp.exp2((m1 - m2) * EXP2_SCALE))
            m, o = lax.fori_loop(0, chunks, more, (
                jnp.full((ROWS, 1), FLOOR, jnp.float32), jnp.zeros((ROWS, 2 * HD), jnp.float32)))
        total = o[:, HD:]
        pout[pl.ds(c * reqs, reqs)] = (o[:, :HD] / total).reshape(reqs, TOK, HEADS, HD)
        plse[pl.ds(pl.multiple_of(c * reqs, reqs), reqs)] = head_lanes(m * EXP2_SCALE + jnp.log2(total), reqs, 0)

    def finish(d):
        out_copy(d, d).wait_recv()
        lse_copy(d, d).wait_recv()

    pl.loop(0, planes)(lambda j: peers(j, finish))

    for i in range(hit_count):
        for r in range(REQUESTS):
            owner = hits[r * hit_count + i]
            rank = jnp.int32(0)
            for r2 in range(r):
                for i2 in range(hit_count):
                    rank = jnp.where(hits[r2 * hit_count + i2] == owner, rank + 1, rank)
            rank = jnp.minimum(rank, CAP - 1)
            comb[i, r] = back[owner, rank]
            row = lback[owner]
            lcomb[i, r:r + 1] = jnp.where(rank == 0, row, pltpu.roll(row, HD // 2, 1))

    top = plse[...]
    for i in range(hit_count):
        top = jnp.maximum(top, lcomb[i])
    share = jnp.exp2(plse[...] - top)
    shares = [jnp.exp2(lcomb[i] - top) for i in range(hit_count)]
    scale = 1.0 / functools.reduce(jnp.add, shares, share)
    whole = (REQUESTS, TOK * HEADS, HD)
    mixed = head_rows(share * scale, REQUESTS) * pout[...].reshape(whole)
    for i in range(hit_count):
        mixed = mixed + head_rows(shares[i] * scale, REQUESTS) * comb[i].reshape(whole).astype(jnp.float32)
    out[...] = mixed.astype(jnp.bfloat16).reshape(PER_DEV, HEADS, HD)

    def drained(d):
        query_copy(d, me).wait_send()
        out_copy(d, me).wait_send()
        lse_copy(d, me).wait_send()

    pl.loop(0, planes)(lambda j: peers(j, drained))
    for t in range(stages):
        kv_copy(t).wait_send()


def solution(mesh):
    n = mesh.shape["cache"]

    def body(prefix_len, hits, span_block, queries, fresh_keys, fresh_values, cache_keys, cache_values):
        hit_count = hits.shape[1]
        vmem = pl.BlockSpec(memory_space=pltpu.VMEM)
        smem = pl.BlockSpec(memory_space=pltpu.SMEM)
        hbm = pl.BlockSpec(memory_space=pltpu.HBM)
        bf16, f32 = jnp.bfloat16, jnp.float32
        dma = pltpu.SemaphoreType.DMA
        block = (n, CAP, TOK, HEADS, HD)
        result = pl.pallas_call(
            functools.partial(kernel, n, hit_count),
            out_shape=jax.ShapeDtypeStruct((PER_DEV, HEADS, HD), bf16),
            in_specs=[smem, smem, vmem, hbm, hbm, hbm, hbm, hbm],
            out_specs=vmem,
            scratch_shapes=[
                pltpu.VMEM((PER_DEV, HEADS * HD), bf16), pltpu.VMEM((REQUESTS, TOK, HEADS, HD), bf16),
                pltpu.VMEM(block, bf16), pltpu.VMEM(block, bf16),
                pltpu.VMEM(block, bf16), pltpu.VMEM(block, bf16),
                pltpu.VMEM((n, 1, HD), f32), pltpu.VMEM((n, 1, HD), f32),
                pltpu.VMEM((n, 2, PER_DEV, HD), bf16),
                pltpu.VMEM((CAP * REGION, HD), bf16), pltpu.VMEM((CAP * REGION, HD), bf16),
                pltpu.VMEM((REQUESTS, TOK, HEADS, HD), f32), pltpu.VMEM((REQUESTS, HD), f32),
                pltpu.VMEM((hit_count, REQUESTS, TOK, HEADS, HD), bf16),
                pltpu.VMEM((hit_count, REQUESTS, HD), f32),
            ] + [dma((n,))] * 6 + [dma((int(math.log2(n)),))] * 2 + [dma((5,))],
            compiler_params=pltpu.CompilerParams(
                collective_id=0, has_side_effects=True, vmem_limit_bytes=60 << 20),
        )(prefix_len, hits.reshape(-1), span_block, queries, fresh_keys, fresh_values, cache_keys, cache_values)
        return result.reshape(PER_DEV, HEADS * HD)

    in_specs = (
        P("groups"), P("groups", None), P("groups", None),
        P(("groups", "cache"), None), P(("groups", "cache"), None), P(("groups", "cache"), None),
        P(("groups", "cache"), None), P(("groups", "cache"), None),
    )
    return jax.shard_map(body, mesh=mesh, in_specs=in_specs,
                         out_specs=P(("groups", "cache"), None), check_vma=False)
```

time: 42.6 us -> 36 us (0.85)
  the two profiles are of different devices: /device:TPU:9 before, /device:TPU:17 now
where the time goes in v2:
time: 36 us; the launch traced here: 35.8 us
  Pallas kernels  34 us (94%)
  local copies, waits for them, and re-layouts  1.72 us (5%)
    pallas_call x1, Pallas kernels, body(): pl.pallas_call(functools.partial(kernel, n, hit_count), out_shape=jax.Sha...  34 us
    unnamed x1, local copies, waits for them, and re-layouts  1.72 us

profile of v2, /device:TPU:17, one launch (start us, length us, event | category | flops | bytes accessed | tf_op | source)
XLA Modules:
  0.0 35.8 jit_solution(9819055139787130652)
XLA Ops:
  0.0 34.0 %shard_map.82 = bf16[64,16,128]{2,1,0:T(8,128)(2,1)} custom-call(s32[16]{0:T(128)} %prefix.1, s32[16]{0:T(128)} %bitcast.6, s32[16,16]{1,0:T(8,128)} %span.1, bf16[64,2048]{1,0:T(8,128)(2,1)} %queries.1, bf16[64,128]{1,0:T(8,128)(2,1)} %fk.1, bf16[64,128]{1,0:T(8,128)(2,1)} %fv.1, bf16[2048,128]{1,0:T(8,128)(2,1)} %ck.1, bf16[2048,128]{1,0:T(8,128)(2,1)} %cv.1), custom_call_target="tpu_custom_call" | custom-call | tf_op jit(solution)/shard_map/pallas_call | solution.py:311
  34.0 1.7 %copy.11 = bf16[8,8,16,128]{3,1,2,0:T(8,128)(2,1)} copy(bf16[8,8,16,128]{3,2,1,0:T(8,128)(2,1)} %bitcast.5) | data formatting | bytes 524288
